TPU v7x, 32 devices: a whole 2x2x4 slice. The times are simulated.
32 devices in a mesh: row: 16 (over z, y, core), col: 2 (over x).
Axes of the slice: x: 2, y: 2, z: 4, core: 2. Of those that a mesh axis runs over, the one named last changes fastest.
Arguments:
- states: bfloat16 [768, 8192], P(None, 'col'), may hold values from -6 to 6
- norm_gain: float32 [8192], P('col'), may hold values from 0.25 to 1.75
- gate_weight: bfloat16 [8192, 28672], P('col', 'row'), may hold values from -0.0625 to 0.0625
- up_weight: bfloat16 [8192, 28672], P('col', 'row'), may hold values from -0.0625 to 0.0625
Outputs:
- near_tiles: float32 [16, 8, 1792, 1792], P('row', 'col')
- far_tiles: float32 [16, 1792, 1792], P('row', 'col')
All inputs are finite; a program needn't handle non-finite values.
Results may differ from a plain program's by a relative error of at most 0.0071.
Values may be sent and summed in bfloat16 or wider, within the bound.
A program may use at most 192 MiB of HBM per device.

v0:
```python
import jax
import jax.numpy as jnp
from jax import lax
from jax.sharding import PartitionSpec as P

D = 8192


def passed_along(shard, axis, by):
    devices = lax.axis_size(axis)
    return lax.ppermute(shard, axis, [(i, (i + by) % devices) for i in range(devices)])


def cross(left, right):
    return lax.dot_general(
        left, right, (((0,), (0,)), ((), ())), preferred_element_type=jnp.float32
    )


def on_device(states, norm_gain, gate_weight, up_weight):
    n_row = lax.axis_size("row")
    n_col = lax.axis_size("col")
    column = lax.axis_index("col")
    width = gate_weight.shape[1]
    count = states.shape[0]
    wide = states.astype(jnp.float32)
    squares = lax.psum(jnp.sum(wide * wide, axis=1), "col")
    inverse = lax.rsqrt(squares / D + 1e-05)
    normed = (wide * inverse[:, None] * norm_gain[None, :]).astype(jnp.bfloat16)
    gate_part = jnp.dot(normed, gate_weight, preferred_element_type=jnp.float32)
    up_part = jnp.dot(normed, up_weight, preferred_element_type=jnp.float32)
    summed = lax.psum_scatter(
        jnp.concatenate([gate_part, up_part], axis=1), "col", scatter_dimension=0, tiled=True
    )
    own_keys = (jax.nn.silu(summed[:, :width]) * summed[:, width:]).astype(jnp.bfloat16)
    keys = lax.all_gather(own_keys, "col", axis=0, tiled=True)
    per_col = n_row // (2 * n_col)
    scale = 1.0 / count
    partner = keys
    for target in range(1, n_col):
        arrived = passed_along(keys, "row", n_row - target * per_col)
        partner = jnp.where(column == target, arrived, partner)
    tiles = [cross(keys, partner) * scale]
    for offset in range(1, per_col):
        partner = passed_along(partner, "row", n_row - 1)
        tiles.append(cross(keys, partner) * scale)
    opposite = passed_along(keys, "row", n_row // 2)
    near_tiles = jnp.stack(tiles, axis=0)[None]
    slab = width // n_col
    own_cols = lax.dynamic_slice_in_dim(keys, column * slab, slab, 1)
    far_tiles = (cross(own_cols, opposite) * scale)[None]
    return (near_tiles, far_tiles)


def solution(mesh):
    placed = (P(None, "col"), P("col"), P("col", "row"), P("col", "row"))
    return jax.shard_map(
        on_device,
        mesh=mesh,
        in_specs=placed,
        out_specs=(P("row", "col", None, None), P("row", "col", None)),
        check_vma=False,
    )
```

profile of v0, /device:TPU:25, one launch (start us, length us, event | category | flops | bytes accessed | tf_op | source)
XLA Modules:
  0.0 585.6 jit_solution(12922400536942425286)
XLA Ops:
  7.2 0.0 reduce-scatter.2.cloned.1.call-start
  7.2 0.0 slice-start
  7.2 4.2 fusion
  11.5 3.8 psum.7
  15.3 0.0 copy-start.2
  15.3 18.4 %fusion.4 = f32[768,1792]{1,0:T(8,128)} fusion(bf16[4096,1792]{1,0:T(8,128)(2,1)} %param.7, bf16[768,4096]{1,0:T(8,128)(2,1)} %param.4, f32[4096]{0:T(1024)S(1)} %copy-done.3, f32[768]{0:T(1024)S(1)} %add_rsqrt_fusion), kind=kOutput, calls=%fused_computation.15 | convolution fusion | flops 11286872064 | bytes 26496000 | tf_op jit(solution)/shard_map/dot_general | solution.py:31
  33.7 13.5 %fusion.6 = f32[768,1792]{1,0:T(8,128)} fusion(bf16[4096,1792]{1,0:T(8,128)(2,1)S(1)} %copy-done.2, bf16[768,4096]{1,0:T(8,128)(2,1)S(1)} %bitcast.24, f32[4096]{0:T(1024)S(1)} %copy-done.3, f32[768]{0:T(1024)S(1)} %add_rsqrt_fusion), kind=kOutput, calls=%fused_computation.16 | convolution fusion | flops 11286872064 | bytes 26496000 | tf_op jit(solution)/shard_map/dot_general | solution.py:30
  47.3 9.7 %pad_maximum_fusion = f32[768,3584]{1,0:T(8,128)} fusion(f32[768,1792]{1,0:T(8,128)} %fusion.4, f32[768,1792]{1,0:T(8,128)} %fusion.6), kind=kLoop, calls=%fused_computation.10 | loop fusion | flops 2752512 | bytes 22020096 | tf_op jit(solution)/shard_map/concatenate | solution.py:33
  56.9 0.0 reduce-scatter.2.cloned.1.call-update
  56.9 0.0 all-gather.2.cloned.1.call-start
  57.0 129.6 %reduce-scatter.2.cloned.1.call-done = f32[384,3584]{1,0:T(8,128)} async-done(((f32[768,3584]{1,0:T(8,128)}), f32[384,3584]{1,0:T(8,128)}) %reduce-scatter.2.cloned.1.call-update) | async-done | bytes 5505040 | tf_op jit(solution)/shard_map/reduce_scatter | solution.py:32
  186.6 4.5 fusion.3
  191.1 0.0 all-gather.2.cloned.1.call-update
  191.1 40.7 %all-gather.2.cloned.1.call-done = bf16[768,1792]{1,0:T(8,128)(2,1)} async-done(((bf16[384,1792]{1,0:T(8,128)(2,1)}), bf16[768,1792]{1,0:T(8,128)(2,1)}) %all-gather.2.cloned.1.call-update) | async-done | bytes 2752528 | tf_op jit(solution)/shard_map/all_gather | solution.py:36
  231.8 0.3 collective-permute-start
  232.0 62.2 %collective-permute-done = bf16[768,1792]{1,0:T(8,128)(2,1)} collective-permute-done((bf16[768,1792]{1,0:T(8,128)(2,1)}, bf16[768,1792]{1,0:T(8,128)(2,1)}, u32[]{:S(2)}, u32[]{:S(2)}) %collective-permute-start) | collective-permute-done | bytes 2752544 | tf_op jit(solution)/shard_map/ppermute | solution.py:11
  294.3 2.1 broadcast_select_fusion
  296.4 0.0 copy-start.1
  296.4 1.7 collective-permute-start.1
  298.1 31.9 %collective-permute-done.1 = bf16[768,1792]{1,0:T(8,128)(2,1)} collective-permute-done((bf16[768,1792]{1,0:T(8,128)(2,1)S(1)}, bf16[768,1792]{1,0:T(8,128)(2,1)}, u32[]{:S(2)}, u32[]{:S(2)}) %collective-permute-start.1) | collective-permute-done | bytes 2752544 | tf_op jit(solution)/shard_map/ppermute | solution.py:11
  330.0 0.0 collective-permute-start.2
  330.1 0.1 collective-permute-start.4
  330.1 32.7 %collective-permute-done.2 = bf16[768,1792]{1,0:T(8,128)(2,1)} collective-permute-done((bf16[768,1792]{1,0:T(8,128)(2,1)}, bf16[768,1792]{1,0:T(8,128)(2,1)}, u32[]{:S(2)}, u32[]{:S(2)}) %collective-permute-start.2) | collective-permute-done | bytes 2752544 | tf_op jit(solution)/shard_map/ppermute | solution.py:11
  362.8 27.3 %collective-permute-start.3 = (bf16[768,1792]{1,0:T(8,128)(2,1)}, bf16[768,1792]{1,0:T(8,128)(2,1)S(1)}, u32[]{:S(2)}, u32[]{:S(2)}) collective-permute-start(bf16[768,1792]{1,0:T(8,128)(2,1)} %collective-permute-done.2), channel_id=1, source_target_pairs={{0,30},{2,0},{4,2},{6,4},{8,6},{10,8},{12,10},{14,12},{16,14},{18,... | collective-permute-start | bytes 8257544 | tf_op jit(solution)/shard_map/ppermute | solution.py:11
  390.2 9.9 %multiply_bitcast_fusion.3 = f32[1,1792,1792]{2,1,0:T(8,128)} fusion(bf16[768,1792]{1,0:T(8,128)(2,1)S(1)} %copy-done, bf16[768,1792]{1,0:T(8,128)(2,1)} %copy-done.1), kind=kOutput, calls=%fused_computation.6 | convolution fusion | flops 4935712768 | bytes 18350080 | tf_op jit(solution)/shard_map/dot_general | solution.py:15
  400.1 109.7 %collective-permute-done.4 = bf16[768,1792]{1,0:T(8,128)(2,1)} collective-permute-done((bf16[768,1792]{1,0:T(8,128)(2,1)S(1)}, bf16[768,1792]{1,0:T(8,128)(2,1)}, u32[]{:S(2)}, u32[]{:S(2)}) %collective-permute-start.4) | collective-permute-done | bytes 2752544 | tf_op jit(solution)/shard_map/ppermute | solution.py:11
  509.8 7.2 %multiply_bitcast_fusion.4 = f32[1,896,1792]{2,1,0:T(8,128)} fusion(bf16[768,1792]{1,0:T(8,128)(2,1)} %collective-permute-done.4, bf16[768,1792]{1,0:T(8,128)(2,1)S(1)} %copy-done, s32[]{:T(128)S(6)} %select_n.13), kind=kOutput, calls=%fused_computation.11 | convolution fusion | flops 2467856384 | bytes 10551300 | tf_op jit(solution)/shard_map/dot_general | solution.py:15
  517.0 9.9 %multiply_bitcast_fusion.2 = f32[1,1792,1792]{2,1,0:T(8,128)} fusion(bf16[768,1792]{1,0:T(8,128)(2,1)S(1)} %copy-done, bf16[768,1792]{1,0:T(8,128)(2,1)} %collective-permute-done.1), kind=kOutput, calls=%fused_computation.5 | convolution fusion | flops 4935712768 | bytes 18350080 | tf_op jit(solution)/shard_map/dot_general | solution.py:15
  526.9 10.0 %multiply_bitcast_fusion.1 = f32[1,1792,1792]{2,1,0:T(8,128)} fusion(bf16[768,1792]{1,0:T(8,128)(2,1)S(1)} %copy-done, bf16[768,1792]{1,0:T(8,128)(2,1)} %collective-permute-done.2), kind=kOutput, calls=%fused_computation.4 | convolution fusion | flops 4935712768 | bytes 18350080 | tf_op jit(solution)/shard_map/dot_general | solution.py:15
  537.0 0.0 collective-permute-done.3
  537.0 8.2 %multiply_bitcast_fusion = f32[1,1792,1792]{2,1,0:T(8,128)} fusion(bf16[768,1792]{1,0:T(8,128)(2,1)S(1)} %copy-done, bf16[768,1792]{1,0:T(8,128)(2,1)S(1)} %collective-permute-done.3), kind=kOutput, calls=%fused_computation.3 | convolution fusion | flops 4935712768 | bytes 18350080 | tf_op jit(solution)/shard_map/dot_general | solution.py:15
  545.2 33.5 %maximum_bitcast_fusion = f32[1,4,1792,1792]{3,2,1,0:T(8,128)} fusion(f32[1,1792,1792]{2,1,0:T(8,128)} %multiply_bitcast_fusion, f32[1,1792,1792]{2,1,0:T(8,128)} %multiply_bitcast_fusion.1, f32[1,1792,1792]{2,1,0:T(8,128)} %multiply_bitcast_fusion.2, f32[1,1792,1792]{2,1,0:T(8,128)} %multiply_bitcast_fusion.3), kind=kLoop, calls=%fused_computation | loop fusion | flops 38535168 | bytes 102760448 | tf_op jit(solution)/shard_map/broadcast_in_dim | solution.py:48
  (11 shorter events, 0.0 us)
Async XLA Ops:
  7.2 8.1 %copy-start.3 = (f32[4096]{0:T(1024)S(1)}, f32[4096]{0:T(1024)}, u32[]{:S(2)}) copy-start(f32[4096]{0:T(1024)} %param.5) | copy-start | bytes 49156
  7.2 179.5 %reduce-scatter.2.cloned.1.call-start = ((), (), s32[]{:S(2)}) async-start(), calls=%async_computation.1 | async-start | bytes 16515072 | tf_op jit(solution)/shard_map/reduce_scatter | solution.py:32
  7.2 26.5 %slice-start = ((s8[6291456]{0:T(1024)(128)(4,1)}), s8[2097152]{0:T(1024)(128)(4,1)S(1)}, s32[]{:S(2)}) async-start(s8[6291456]{0:T(1024)(128)(4,1)} %bitcast.23), calls=%async_computation.3 | async-start | bytes 4194304
  15.2 18.5 %slice-start.1 = ((s8[6291456]{0:T(1024)(128)(4,1)}), s8[4194304]{0:T(1024)(128)(4,1)S(1)}, s32[]{:S(2)}) async-start(s8[6291456]{0:T(1024)(128)(4,1)} %bitcast.23), calls=%async_computation.4 | async-start | bytes 8388608
  15.3 18.5 %copy-start.2 = (bf16[4096,1792]{1,0:T(8,128)(2,1)S(1)}, bf16[4096,1792]{1,0:T(8,128)(2,1)}, u32[]{:S(2)}) copy-start(bf16[4096,1792]{1,0:T(8,128)(2,1)} %param.6) | copy-start | bytes 44040196
  56.9 174.8 %all-gather.2.cloned.1.call-start = ((), (), s32[]{:S(2)}) async-start(), calls=%async_computation.2 | async-start | bytes 4128768 | tf_op jit(solution)/shard_map/all_gather | solution.py:36
  231.8 98.3 %copy-start = (bf16[768,1792]{1,0:T(8,128)(2,1)S(1)}, bf16[768,1792]{1,0:T(8,128)(2,1)}, u32[]{:S(2)}) copy-start(bf16[768,1792]{1,0:T(8,128)(2,1)} %all-gather.2.cloned.1.call-done) | copy-start | bytes 8257540
  231.8 62.5 %collective-permute-start = (bf16[768,1792]{1,0:T(8,128)(2,1)}, bf16[768,1792]{1,0:T(8,128)(2,1)}, u32[]{:S(2)}, u32[]{:S(2)}) collective-permute-start(bf16[768,1792]{1,0:T(8,128)(2,1)} %all-gather.2.cloned.1.call-done), channel_id=1, source_target_pairs={{0,24},{2,26},{4,28},{6,30},{8,0},{10,2},{12,4},{14,6},{16,8},{18,... | collective-permute-start | bytes 8257544 | tf_op jit(solution)/shard_map/ppermute | solution.py:11
  296.4 33.7 %copy-start.1 = (bf16[768,1792]{1,0:T(8,128)(2,1)}, bf16[768,1792]{1,0:T(8,128)(2,1)S(1)}, u32[]{:S(2)}) copy-start(bf16[768,1792]{1,0:T(8,128)(2,1)S(1)} %broadcast_select_fusion) | copy-start | bytes 8257540
  296.4 33.7 %collective-permute-start.1 = (bf16[768,1792]{1,0:T(8,128)(2,1)S(1)}, bf16[768,1792]{1,0:T(8,128)(2,1)}, u32[]{:S(2)}, u32[]{:S(2)}) collective-permute-start(bf16[768,1792]{1,0:T(8,128)(2,1)S(1)} %broadcast_select_fusion), channel_id=1, source_target_pairs={{0,30},{2,0},{4,2},{6,4},{8,6},{10,8},{12,10},{14,12},{16,14},{18,... | collective-permute-start | bytes 8257544 | tf_op jit(solution)/shard_map/ppermute | solution.py:11
  330.0 32.8 %collective-permute-start.2 = (bf16[768,1792]{1,0:T(8,128)(2,1)}, bf16[768,1792]{1,0:T(8,128)(2,1)}, u32[]{:S(2)}, u32[]{:S(2)}) collective-permute-start(bf16[768,1792]{1,0:T(8,128)(2,1)} %collective-permute-done.1), channel_id=1, source_target_pairs={{0,30},{2,0},{4,2},{6,4},{8,6},{10,8},{12,10},{14,12},{16,14},{18,... | collective-permute-start | bytes 8257544 | tf_op jit(solution)/shard_map/ppermute | solution.py:11
  330.1 179.7 %collective-permute-start.4 = (bf16[768,1792]{1,0:T(8,128)(2,1)S(1)}, bf16[768,1792]{1,0:T(8,128)(2,1)}, u32[]{:S(2)}, u32[]{:S(2)}) collective-permute-start(bf16[768,1792]{1,0:T(8,128)(2,1)S(1)} %copy-done), channel_id=1, source_target_pairs={{0,16},{2,18},{4,20},{6,22},{8,24},{10,26},{12,28},{14,30},{16,0},... | collective-permute-start | bytes 8257544 | tf_op jit(solution)/shard_map/ppermute | solution.py:11
  362.8 174.1 %collective-permute-start.3 = (bf16[768,1792]{1,0:T(8,128)(2,1)}, bf16[768,1792]{1,0:T(8,128)(2,1)S(1)}, u32[]{:S(2)}, u32[]{:S(2)}) collective-permute-start(bf16[768,1792]{1,0:T(8,128)(2,1)} %collective-permute-done.2), channel_id=1, source_target_pairs={{0,30},{2,0},{4,2},{6,4},{8,6},{10,8},{12,10},{14,12},{16,14},{18,... | collective-permute-start | bytes 8257544 | tf_op jit(solution)/shard_map/ppermute | solution.py:11
Sparse Core Ops, SparseCore 0:
  57.1 129.5 reduce-scatter.1
  191.2 40.4 all-gather.1
where the time goes:
time: 586 us
  waiting for transfers between devices  407 us (69%)
  matrix products  77.2 us (13%)
  other arithmetic  54 us (9%)
  starting transfers between devices  29.5 us (5%)
  between operations  14.1 us (2%)
    ppermute x5, waiting for transfers between devices, passed_along(): lax.ppermute(shard, axis, [(i, (i + by) % devices) for i in range(devices)])  237 us
    reduce_scatter x1, waiting for transfers between devices, on_device(): lax.psum_scatter(jnp.concatenate([gate_part, up_part], axis=1), 'col', sc...  130 us
    dot_general x5, matrix products, cross(): lax.dot_general(left, right, (((0,), (0,)), ((), ())), preferred_element_...  45.3 us
    all_gather x1, waiting for transfers between devices, on_device(): keys = lax.all_gather(own_keys, 'col', axis=0, tiled=True)  40.7 us
    broadcast_in_dim x1, other arithmetic, on_device(): near_tiles = jnp.stack(tiles, axis=0)[None]  33.5 us
    ppermute x5, starting transfers between devices, passed_along(): lax.ppermute(shard, axis, [(i, (i + by) % devices) for i in range(devices)])  29.4 us
    dot_general x1, matrix products, on_device(): up_part = jnp.dot(normed, up_weight, preferred_element_type=jnp.float32)  18.4 us
    dot_general x1, matrix products, on_device(): gate_part = jnp.dot(normed, gate_weight, preferred_element_type=jnp.float32)  13.5 us
  transfers between devices with their start and end apart: 7, of which 6 were waited for; matrix products, arithmetic and copies ran while one was open for 6% of the time, Pallas kernels for 0%

commit v1 on v0

--- a/solution.py
+++ b/solution.py
@@ -1,9 +1,17 @@
+import functools
+
 import jax
 import jax.numpy as jnp
 from jax import lax
+from jax.experimental import pallas as pl
+from jax.experimental.pallas import tpu as pltpu
 from jax.sharding import PartitionSpec as P
 
-D = 8192
+LANES = 128
+GROUP = 2
+MESH = pl.DeviceIdType.MESH
+SUM, PAIR, NEXT_OWN, NEXT_OTHER, PREV_OWN, HALF_OWN, HALF_OTHER, SIDE, CORE_ODD, CORE_TOP = range(10)
+OWN, STEP, OPPOSITE, BASE1, BASE2, BASE3, BEHIND = range(7)
 
 
 def passed_along(shard, axis, by):
@@ -15,6 +23,255 @@
     return lax.dot_general(
         left, right, (((0,), (0,)), ((), ())), preferred_element_type=jnp.float32
     )
+
+
+def gather_kernel(n_row, step, x_ref, gate_hbm, up_hbm, kept, wbuf, partial, sent, got, mine,
+                  w_sem, local_sem, send_sem, recv_sem):
+    row = lax.axis_index("row")
+    col = lax.axis_index("col")
+    core = lax.rem(row, 2)
+    y = lax.rem(lax.div(row, 2), 2)
+    chunks, half, wide = sent.shape
+    cut = wide // 2
+    group = cut // LANES
+    own_rows = pl.ds(pl.multiple_of(col * half, half), half)
+    other_rows = pl.ds(pl.multiple_of((1 - col) * half, half), half)
+
+    pair = (row, 1 - col)
+    before = (lax.rem(row + n_row - step, n_row), col)
+    after = (lax.rem(row + step, n_row), col)
+    side = (row + 2 - 4 * y, col)
+    twin = (row + 1 - 2 * core, col)
+
+    def weights(j, slot):
+        cols = pl.ds(pl.multiple_of(j * cut, cut), cut)
+        return (
+            pltpu.make_async_copy(gate_hbm.at[:, cols], wbuf.at[slot, :, pl.ds(0, cut)], w_sem.at[slot, 0]),
+            pltpu.make_async_copy(up_hbm.at[:, cols], wbuf.at[slot, :, pl.ds(cut, cut)], w_sem.at[slot, 1]),
+        )
+
+    def part(slot, j, rows=None):
+        where = pl.ds(j * group, group)
+        return kept.at[slot, where] if rows is None else kept.at[slot, where, rows]
+
+    def remote(kind, j, src, dst, to):
+        return pltpu.make_async_remote_copy(
+            src_ref=src, dst_ref=dst, send_sem=send_sem.at[kind, j], recv_sem=recv_sem.at[kind, j],
+            device_id=to, device_id_type=MESH,
+        )
+
+    def copies(j):
+        made = {
+            SUM: (sent.at[j], got.at[j], pair),
+            PAIR: (mine.at[j], part(OWN, j, own_rows), pair),
+            NEXT_OWN: (mine.at[j], part(STEP, j, own_rows), before),
+            NEXT_OTHER: (part(OWN, j, other_rows), part(STEP, j, other_rows), before),
+            PREV_OWN: (mine.at[j], part(BEHIND, j, own_rows), after),
+            HALF_OWN: (part(BEHIND, j, own_rows), part(OPPOSITE, j, own_rows), after),
+            HALF_OTHER: (part(STEP, j, other_rows), part(OPPOSITE, j, other_rows), before),
+            SIDE: (part(col + 1 - y, j), part(BASE2, j), side),
+            CORE_ODD: (part(BASE2 * (1 - core) + col * core, j), part(BASE1, j), twin),
+            CORE_TOP: (part((col + 1) * (1 - core) + BASE2 * core, j), part(BASE3, j), twin),
+        }
+        return {kind: functools.partial(remote, kind, j, *ends) for kind, ends in made.items()}
+
+    def local(j):
+        return pltpu.make_async_copy(mine.at[j], part(OWN, j, own_rows), local_sem.at[j])
+
+    for copy in weights(0, 0):
+        copy.start()
+    barrier = pltpu.get_barrier_semaphore()
+    for device in (pair, before, after, side, twin):
+        pl.semaphore_signal(barrier, inc=1, device_id=device, device_id_type=MESH)
+    pl.semaphore_wait(barrier, 5)
+
+    def stage(t, lag, act):
+        j = t - lag
+
+        @pl.when(jnp.logical_and(j >= 0, j < chunks))
+        def _():
+            act(j, copies(j))
+
+    def multiply(j, copy):
+        slot = lax.rem(j, 2)
+        for w in weights(j, slot):
+            w.wait()
+
+        @pl.when(j + 1 < chunks)
+        def _():
+            for w in weights(j + 1, 1 - slot):
+                w.start()
+
+        sent[j] = jnp.dot(
+            x_ref[other_rows, :], wbuf[slot], preferred_element_type=jnp.float32
+        ).astype(jnp.bfloat16)
+        copy[SUM]().start()
+        partial[slot] = jnp.dot(x_ref[own_rows, :], wbuf[slot], preferred_element_type=jnp.float32)
+
+    def activate(j, copy):
+        copy[SUM]().wait_recv()
+        total = partial[lax.rem(j, 2)] + got[j].astype(jnp.float32)
+        gate = total[:, :cut]
+        keys = (gate / (1.0 + jnp.exp(-gate)) * total[:, cut:]).astype(jnp.bfloat16)
+        for s in range(group):
+            mine[j, s] = keys[:, s * LANES:(s + 1) * LANES]
+        copy[PAIR]().start()
+        copy[NEXT_OWN]().start()
+        copy[PREV_OWN]().start()
+        local(j).start()
+
+    def spread(j, copy):
+        copy[PAIR]().wait_recv()
+        copy[NEXT_OTHER]().start()
+        copy[PREV_OWN]().wait_recv()
+        copy[HALF_OWN]().start()
+
+    def further(j, copy):
+        copy[NEXT_OTHER]().wait_recv()
+        copy[HALF_OTHER]().start()
+        copy[NEXT_OWN]().wait_recv()
+        local(j).wait()
+
+    def sideways(j, copy):
+        copy[HALF_OWN]().wait_recv()
+        copy[HALF_OTHER]().wait_recv()
+        copy[SIDE]().start()
+
+    def within(j, copy):
+        copy[SIDE]().wait_recv()
+        copy[CORE_ODD]().start()
+        copy[CORE_TOP]().start()
+
+    def arrive(j, copy):
+        copy[CORE_ODD]().wait_recv()
+        copy[CORE_TOP]().wait_recv()
+        for kind in copy:
+            copy[kind]().wait_send()
+
+    @pl.loop(0, chunks + 6)
+    def _(t):
+        stage(t, 0, multiply)
+        stage(t, 1, activate)
+        stage(t, 2, spread)
+        stage(t, 3, further)
+        stage(t, 4, sideways)
+        stage(t, 5, within)
+        stage(t, 6, arrive)
+
+
+def gather_keys(n_row, step, normed, gate_weight, up_weight):
+    count, depth = normed.shape
+    width = gate_weight.shape[1]
+    cut = GROUP * LANES
+    chunks = width // cut
+    half = count // 2
+    return pl.pallas_call(
+        functools.partial(gather_kernel, n_row, step),
+        out_shape=jax.ShapeDtypeStruct((7, width // LANES, count, LANES), jnp.bfloat16),
+        in_specs=[
+            pl.BlockSpec(memory_space=pltpu.VMEM),
+            pl.BlockSpec(memory_space=pl.ANY),
+            pl.BlockSpec(memory_space=pl.ANY),
+        ],
+        out_specs=pl.BlockSpec(memory_space=pl.ANY),
+        scratch_shapes=[
+            pltpu.VMEM((2, depth, 2 * cut), jnp.bfloat16),
+            pltpu.VMEM((2, half, 2 * cut), jnp.float32),
+            pltpu.VMEM((chunks, half, 2 * cut), jnp.bfloat16),
+            pltpu.VMEM((chunks, half, 2 * cut), jnp.bfloat16),
+            pltpu.VMEM((chunks, GROUP, half, LANES), jnp.bfloat16),
+            pltpu.SemaphoreType.DMA((2, 2)),
+            pltpu.SemaphoreType.DMA((chunks,)),
+            pltpu.SemaphoreType.DMA((10, chunks)),
+            pltpu.SemaphoreType.DMA((10, chunks)),
+        ],
+        compiler_params=pltpu.CompilerParams(
+            collective_id=0, has_side_effects=True, vmem_limit_bytes=56 * 2**20
+        ),
+        name="gather_keys",
+    )(normed, gate_weight, up_weight)
+
+
+def tiles_kernel(scale, col_ref, left_ref, right_ref, near_ref, far_ref, turned):
+    s = pl.program_id(0)
+    last = pl.num_programs(0) - 1
+    blocks = left_ref.shape[1]
+    slab = far_ref.shape[1]
+
+    @pl.when(s == 0)
+    def _():
+        for b in range(blocks):
+            turned[b * LANES:(b + 1) * LANES, :] = left_ref[0, b].T
+
+    def fill(out_ref, start):
+        rows = turned[pl.ds(pl.multiple_of(start, slab), slab), :]
+        for b in range(0, blocks, 2):
+            right = jnp.concatenate([right_ref[0, b], right_ref[0, b + 1]], axis=1)
+            out_ref[:, b * LANES:(b + 2) * LANES] = (
+                jnp.dot(rows, right, preferred_element_type=jnp.float32) * scale
+            )
+
+    @pl.when(s < last)
+    def _():
+        fill(near_ref.at[0, 0], lax.rem(s, 2) * slab)
+
+    @pl.when(s == last)
+    def _():
+        fill(far_ref.at[0], col_ref[0] * slab)
+
+
+def tiles(kept, col, per_col, scale):
+    _, blocks, count, _ = kept.shape
+    width = blocks * LANES
+    slab = width // 2
+    steps = 2 * per_col + 1
+
+    def block_of(s, col_ref):
+        m = lax.div(s, 2)
+        near = jnp.where(m == 0, col_ref[0], OPPOSITE + m)
+        return jnp.where(s == steps - 1, OPPOSITE, near)
+
+    def place_of(s):
+        return jnp.minimum(s, steps - 2)
+
+    return pl.pallas_call(
+        functools.partial(tiles_kernel, scale),
+        grid_spec=pltpu.PrefetchScalarGridSpec(
+            num_scalar_prefetch=1,
+            grid=(steps,),
+            in_specs=[
+                pl.BlockSpec((1, blocks, count, LANES), lambda s, c: (OWN, 0, 0, 0)),
+                pl.BlockSpec((1, blocks, count, LANES), lambda s, c: (block_of(s, c), 0, 0, 0)),
+            ],
+            out_specs=[
+                pl.BlockSpec((1, 1, slab, width),
+                             lambda s, c: (0, lax.div(place_of(s), 2), lax.rem(place_of(s), 2), 0)),
+                pl.BlockSpec((1, slab, width), lambda s, c: (0, 0, 0)),
+            ],
+            scratch_shapes=[pltpu.VMEM((width, count), jnp.bfloat16)],
+        ),
+        out_shape=(
+            jax.ShapeDtypeStruct((1, per_col, width, width), jnp.float32),
+            jax.ShapeDtypeStruct((1, slab, width), jnp.float32),
+        ),
+        compiler_params=pltpu.CompilerParams(
+            dimension_semantics=("arbitrary",), vmem_limit_bytes=56 * 2**20
+        ),
+        name="tiles",
+    )(col.reshape(1).astype(jnp.int32), kept, kept)
+
+
+def by_routes(states, norm_gain, gate_weight, up_weight):
+    n_row = lax.axis_size("row")
+    n_col = lax.axis_size("col")
+    per_col = n_row // (2 * n_col)
+    features = states.shape[1] * n_col
+    wide = states.astype(jnp.float32)
+    squares = lax.psum(jnp.sum(wide * wide, axis=1), "col")
+    inverse = lax.rsqrt(squares / features + 1e-05)
+    normed = (wide * inverse[:, None] * norm_gain[None, :]).astype(jnp.bfloat16)
+    kept = gather_keys(n_row, per_col, normed, gate_weight, up_weight)
+    return tiles(kept, lax.axis_index("col"), per_col, 1.0 / states.shape[0])
 
 
 def on_device(states, norm_gain, gate_weight, up_weight):
@@ -25,7 +282,7 @@
     count = states.shape[0]
     wide = states.astype(jnp.float32)
     squares = lax.psum(jnp.sum(wide * wide, axis=1), "col")
-    inverse = lax.rsqrt(squares / D + 1e-05)
+    inverse = lax.rsqrt(squares / (states.shape[1] * n_col) + 1e-05)
     normed = (wide * inverse[:, None] * norm_gain[None, :]).astype(jnp.bfloat16)
     gate_part = jnp.dot(normed, gate_weight, preferred_element_type=jnp.float32)
     up_part = jnp.dot(normed, up_weight, preferred_element_type=jnp.float32)
@@ -52,12 +309,23 @@
     return (near_tiles, far_tiles)
 
 
+def fits(mesh, states, gate_weight):
+    n_row, n_col = mesh.shape["row"], mesh.shape["col"]
+    width = gate_weight.shape[1] // n_row
+    return n_col == 2 and n_row == 8 * n_col and width % (2 * GROUP * LANES // 2) == 0 and states.shape[0] % 32 == 0
+
+
 def solution(mesh):
     placed = (P(None, "col"), P("col"), P("col", "row"), P("col", "row"))
-    return jax.shard_map(
-        on_device,
-        mesh=mesh,
-        in_specs=placed,
-        out_specs=(P("row", "col", None, None), P("row", "col", None)),
-        check_vma=False,
-    )
+
+    def program(states, norm_gain, gate_weight, up_weight):
+        on_each = by_routes if fits(mesh, states, gate_weight) else on_device
+        return jax.shard_map(
+            on_each,
+            mesh=mesh,
+            in_specs=placed,
+            out_specs=(P("row", "col", None, None), P("row", "col", None)),
+            check_vma=False,
+        )(states, norm_gain, gate_weight, up_weight)
+
+    return program

time: 586 us -> 241 us (0.41)
  waiting for transfers between devices: 407 us -> 0 us
  Pallas kernels: 0 us -> 220 us
  matrix products: 77.2 us -> 0 us
  other arithmetic: 54 us -> 12.1 us
  starting transfers between devices: 29.5 us -> 0 us
  between operations: 14.1 us -> 0.64 us
    ppermute x5 -> x0, waiting for transfers between devices: 237 us -> none  [passed_along(): lax.ppermute(shard, axis, [(i, (i + by) % devices) for i in range(devices)])]
    pallas_call x0 -> x2, Pallas kernels: none -> 220 us  [the longest x1 182 us: gather_keys(): pl.pallas_call(functools.partial(gather_kernel, n_row, step), out_shape=j...]
    reduce_scatter x1 -> x0, waiting for transfers between devices: 130 us -> none  [on_device(): lax.psum_scatter(jnp.concatenate([gate_part, up_part], axis=1), 'col', sc...]
    dot_general x7 -> x0, matrix products: 77.2 us -> none  [the longest x5 45.3 us: cross(): lax.dot_general(left, right, (((0,), (0,)), ((), ())), preferred_element_...]
    all_gather x1 -> x0, waiting for transfers between devices: 40.7 us -> none  [on_device(): keys = lax.all_gather(own_keys, 'col', axis=0, tiled=True)]
    broadcast_in_dim x1 -> x0, other arithmetic: 33.5 us -> none  [on_device(): near_tiles = jnp.stack(tiles, axis=0)[None]]
    ppermute x5 -> x0, starting transfers between devices: 29.4 us -> none  [passed_along(): lax.ppermute(shard, axis, [(i, (i + by) % devices) for i in range(devices)])]
    concatenate x1 -> x0, other arithmetic: 9.66 us -> none  [on_device(): jnp.concatenate([gate_part, up_part], axis=1)]
  transfers between devices with their start and end apart: 7 -> 0, of which waited for: 6 -> 0; matrix products, arithmetic and copies ran while one was open for 6% -> 0% of each run, Pallas kernels for 0% -> 0%
where the time goes in v1:
time: 241 us; the launch traced here: 236 us
  Pallas kernels  220 us (91%)
  other arithmetic  12.1 us (5%)
  blocking collectives  3.78 us (2%)
    pallas_call x1, Pallas kernels, gather_keys(): pl.pallas_call(functools.partial(gather_kernel, n_row, step), out_shape=j...  182 us
    pallas_call x1, Pallas kernels, tiles(): pl.pallas_call(functools.partial(tiles_kernel, scale), grid_spec=pltpu.Pr...  37.1 us
    convert_element_type x1, other arithmetic, by_routes(): normed = (wide * inverse[:, None] * norm_gain[None, :]).astype(jnp.bfloat16)  8.04 us

profile of v1, /device:TPU:25, one launch (start us, length us, event | category | flops | bytes accessed | tf_op | source)
XLA Modules:
  0.0 236.1 jit_solution(9097737557869050014)
XLA Ops:
  0.6 4.1 %fusion = f32[768]{0:T(1024)S(1)} fusion(bf16[768,4096]{1,0:T(8,128)(2,1)} %param.4), kind=kLoop, calls=%fused_computation.2 | loop fusion | flops 9436416 | bytes 6294528 | tf_op jit(solution)/shard_map/reduce_sum | solution.py:270
  4.7 3.8 %psum.7 = f32[768]{0:T(1024)S(1)} all-reduce(f32[768]{0:T(1024)S(1)} %fusion), channel_id=1, replica_groups=mesh['row'=16,'col'=2] {'col'}, use_global_device_ids=true, to_apply=%region_1.0 | all-reduce | flops 768 | bytes 6144 | tf_op jit(solution)/shard_map/psum | solution.py:270
  8.5 8.0 %fusion.2.x_ref = bf16[768,4096]{1,0:T(8,128)(2,1)} fusion(bf16[768,4096]{1,0:T(8,128)(2,1)} %param.4, f32[4096]{0:T(1024)} %param.5, f32[768]{0:T(1024)S(1)} %add_rsqrt_fusion), kind=kLoop, calls=%fused_computation.4 | loop fusion | flops 12582912 | bytes 12602368 | tf_op jit(solution)/shard_map/convert_element_type | solution.py:272
  16.5 182.4 %gather_keys.1.left_ref.right_ref = bf16[7,14,768,128]{3,2,1,0:T(8,128)(2,1)} custom-call(bf16[768,4096]{1,0:T(8,128)(2,1)} %fusion.2.x_ref, bf16[4096,1792]{1,0:T(8,128)(2,1)} %gate_hbm.1, bf16[4096,1792]{1,0:T(8,128)(2,1)} %up_hbm.1), custom_call_target="tpu_custom_call" | custom-call | tf_op jit(solution)/shard_map/gather_keys/pallas_call | solution.py:168
  198.9 37.1 %tiles.1 = (f32[1,4,1792,1792]{3,2,1,0:T(8,128)}, f32[1,896,1792]{2,1,0:T(8,128)}) custom-call(s32[1]{0:T(128)} %bitcast.col_ref, bf16[7,14,768,128]{3,2,1,0:T(8,128)(2,1)} %gather_keys.1.left_ref.right_ref, bf16[7,14,768,128]{3,2,1,0:T(8,128)(2,1)} %gather_keys.1.left_ref.right_ref), custom_call_target="tpu_custom_call" | custom-call | tf_op jit(solution)/shard_map/tiles/pallas_call | solution.py:237
  (1 shorter events, 0.0 us)

commit v2 on v1

--- a/solution.py
+++ b/solution.py
@@ -8,10 +8,11 @@
 from jax.sharding import PartitionSpec as P
 
 LANES = 128
-GROUP = 2
+GROUP = 1
 MESH = pl.DeviceIdType.MESH
-SUM, PAIR, NEXT_OWN, NEXT_OTHER, PREV_OWN, HALF_OWN, HALF_OTHER, SIDE, CORE_ODD, CORE_TOP = range(10)
-OWN, STEP, OPPOSITE, BASE1, BASE2, BASE3, BEHIND = range(7)
+(SUM, PAIR, NEXT_OWN, NEXT_OTHER, FAR_OWN, FAR_OTHER, RELAY_OWN, RELAY_OTHER,
+ LAST_OWN, LAST_OTHER, SIDE, CORE_ODD, CORE_TOP) = range(13)
+OWN, STEP, OPPOSITE, BASE1, BASE2, BASE3 = range(6)
 
 
 def passed_along(shard, axis, by):
@@ -38,8 +39,10 @@
     other_rows = pl.ds(pl.multiple_of((1 - col) * half, half), half)
 
     pair = (row, 1 - col)
-    before = (lax.rem(row + n_row - step, n_row), col)
-    after = (lax.rem(row + step, n_row), col)
+    level = lax.div(row, step)
+    below = (lax.rem(row + n_row - step, n_row), col)
+    above = (lax.rem(row + step, n_row), col)
+    two_off = (lax.rem(row + 2 * step, n_row), col)
     side = (row + 2 - 4 * y, col)
     twin = (row + 1 - 2 * core, col)
 
@@ -64,11 +67,14 @@
         made = {
             SUM: (sent.at[j], got.at[j], pair),
             PAIR: (mine.at[j], part(OWN, j, own_rows), pair),
-            NEXT_OWN: (mine.at[j], part(STEP, j, own_rows), before),
-            NEXT_OTHER: (part(OWN, j, other_rows), part(STEP, j, other_rows), before),
-            PREV_OWN: (mine.at[j], part(BEHIND, j, own_rows), after),
-            HALF_OWN: (part(BEHIND, j, own_rows), part(OPPOSITE, j, own_rows), after),
-            HALF_OTHER: (part(STEP, j, other_rows), part(OPPOSITE, j, other_rows), before),
+            NEXT_OWN: (mine.at[j], part(STEP, j, own_rows), below),
+            NEXT_OTHER: (part(OWN, j, other_rows), part(STEP, j, other_rows), below),
+            FAR_OWN: (mine.at[j], part(OPPOSITE, j, own_rows), two_off),
+            FAR_OTHER: (part(OWN, j, other_rows), part(OPPOSITE, j, other_rows), two_off),
+            RELAY_OWN: (part(STEP, j, own_rows), part(OPPOSITE, j, own_rows), below),
+            RELAY_OTHER: (part(STEP, j, other_rows), part(OPPOSITE, j, other_rows), below),
+            LAST_OWN: (part(OPPOSITE, j, own_rows), part(STEP, j, own_rows), above),
+            LAST_OTHER: (part(OPPOSITE, j, other_rows), part(STEP, j, other_rows), above),
             SIDE: (part(col + 1 - y, j), part(BASE2, j), side),
             CORE_ODD: (part(BASE2 * (1 - core) + col * core, j), part(BASE1, j), twin),
             CORE_TOP: (part((col + 1) * (1 - core) + BASE2 * core, j), part(BASE3, j), twin),
@@ -81,9 +87,9 @@
     for copy in weights(0, 0):
         copy.start()
     barrier = pltpu.get_barrier_semaphore()
-    for device in (pair, before, after, side, twin):
+    for device in (pair, below, above, two_off, side, twin):
         pl.semaphore_signal(barrier, inc=1, device_id=device, device_id_type=MESH)
-    pl.semaphore_wait(barrier, 5)
+    pl.semaphore_wait(barrier, 6)
 
     def stage(t, lag, act):
         j = t - lag
@@ -116,25 +122,53 @@
         for s in range(group):
             mine[j, s] = keys[:, s * LANES:(s + 1) * LANES]
         copy[PAIR]().start()
-        copy[NEXT_OWN]().start()
-        copy[PREV_OWN]().start()
+        start(copy, NEXT_OWN)
+        start(copy, FAR_OWN)
         local(j).start()
+
+    senders = {
+        NEXT_OWN: level >= 1, NEXT_OTHER: level >= 1,
+        FAR_OWN: level <= 1, FAR_OTHER: level <= 1,
+        RELAY_OWN: jnp.logical_or(level == 1, level == 2),
+        RELAY_OTHER: jnp.logical_or(level == 1, level == 2),
+        LAST_OWN: level == 2, LAST_OTHER: level == 2,
+    }
+    receivers = {
+        NEXT_OWN: level <= 2, NEXT_OTHER: level <= 2,
+        FAR_OWN: level >= 2, FAR_OTHER: level >= 2,
+        RELAY_OWN: level <= 1, RELAY_OTHER: level <= 1,
+        LAST_OWN: level == 3, LAST_OTHER: level == 3,
+    }
+
+    def start(copy, kind):
+        pl.when(senders[kind])(lambda: copy[kind]().start())
+
+    def receive(copy, kind):
+        pl.when(receivers[kind])(lambda: copy[kind]().wait_recv())
 
     def spread(j, copy):
         copy[PAIR]().wait_recv()
-        copy[NEXT_OTHER]().start()
-        copy[PREV_OWN]().wait_recv()
-        copy[HALF_OWN]().start()
+        start(copy, NEXT_OTHER)
+        start(copy, FAR_OTHER)
+        receive(copy, NEXT_OWN)
+        start(copy, RELAY_OWN)
 
     def further(j, copy):
-        copy[NEXT_OTHER]().wait_recv()
-        copy[HALF_OTHER]().start()
-        copy[NEXT_OWN]().wait_recv()
+        receive(copy, NEXT_OTHER)
+        start(copy, RELAY_OTHER)
+        receive(copy, FAR_OWN)
+        start(copy, LAST_OWN)
+
+    def onward(j, copy):
+        receive(copy, FAR_OTHER)
+        start(copy, LAST_OTHER)
+        receive(copy, RELAY_OWN)
         local(j).wait()
 
     def sideways(j, copy):
-        copy[HALF_OWN]().wait_recv()
-        copy[HALF_OTHER]().wait_recv()
+        receive(copy, RELAY_OTHER)
+        receive(copy, LAST_OWN)
+        receive(copy, LAST_OTHER)
         copy[SIDE]().start()
 
     def within(j, copy):
@@ -146,17 +180,21 @@
         copy[CORE_ODD]().wait_recv()
         copy[CORE_TOP]().wait_recv()
         for kind in copy:
-            copy[kind]().wait_send()
-
-    @pl.loop(0, chunks + 6)
+            if kind in senders:
+                pl.when(senders[kind])(lambda kind=kind: copy[kind]().wait_send())
+            else:
+                copy[kind]().wait_send()
+
+    @pl.loop(0, chunks + 7)
     def _(t):
         stage(t, 0, multiply)
         stage(t, 1, activate)
         stage(t, 2, spread)
         stage(t, 3, further)
-        stage(t, 4, sideways)
-        stage(t, 5, within)
-        stage(t, 6, arrive)
+        stage(t, 4, onward)
+        stage(t, 5, sideways)
+        stage(t, 6, within)
+        stage(t, 7, arrive)
 
 
 def gather_keys(n_row, step, normed, gate_weight, up_weight):
@@ -167,7 +205,7 @@
     half = count // 2
     return pl.pallas_call(
         functools.partial(gather_kernel, n_row, step),
-        out_shape=jax.ShapeDtypeStruct((7, width // LANES, count, LANES), jnp.bfloat16),
+        out_shape=jax.ShapeDtypeStruct((6, width // LANES, count, LANES), jnp.bfloat16),
         in_specs=[
             pl.BlockSpec(memory_space=pltpu.VMEM),
             pl.BlockSpec(memory_space=pl.ANY),
@@ -182,8 +220,8 @@
             pltpu.VMEM((chunks, GROUP, half, LANES), jnp.bfloat16),
             pltpu.SemaphoreType.DMA((2, 2)),
             pltpu.SemaphoreType.DMA((chunks,)),
-            pltpu.SemaphoreType.DMA((10, chunks)),
-            pltpu.SemaphoreType.DMA((10, chunks)),
+            pltpu.SemaphoreType.DMA((13, chunks)),
+            pltpu.SemaphoreType.DMA((13, chunks)),
         ],
         compiler_params=pltpu.CompilerParams(
             collective_id=0, has_side_effects=True, vmem_limit_bytes=56 * 2**20
@@ -312,7 +350,7 @@
 def fits(mesh, states, gate_weight):
     n_row, n_col = mesh.shape["row"], mesh.shape["col"]
     width = gate_weight.shape[1] // n_row
-    return n_col == 2 and n_row == 8 * n_col and width % (2 * GROUP * LANES // 2) == 0 and states.shape[0] % 32 == 0
+    return n_col == 2 and n_row == 8 * n_col and width % (2 * LANES) == 0 and states.shape[0] % 32 == 0
 
 
 def solution(mesh):

time: 241 us -> 215 us (0.89); the launches traced: 236 us -> 215 us
  Pallas kernels: 220 us -> 198 us
    pallas_call x1, Pallas kernels: 182 us -> 161 us  [gather_keys(): pl.pallas_call(functools.partial(gather_kernel, n_row, step), out_shape=j...]
where the time goes in v2:
time: 215 us
  Pallas kernels  198 us (92%)
  other arithmetic  12.1 us (6%)
  blocking collectives  3.78 us (2%)
    pallas_call x1, Pallas kernels, gather_keys(): pl.pallas_call(functools.partial(gather_kernel, n_row, step), out_shape=j...  161 us
    pallas_call x1, Pallas kernels, tiles(): pl.pallas_call(functools.partial(tiles_kernel, scale), grid_spec=pltpu.Pr...  37.1 us
    convert_element_type x1, other arithmetic, by_routes(): normed = (wide * inverse[:, None] * norm_gain[None, :]).astype(jnp.bfloat16)  8.04 us

profile of v2, /device:TPU:25, one launch (start us, length us, event | category | flops | bytes accessed | tf_op | source)
XLA Modules:
  0.0 214.5 jit_solution(8504540815435387183)
XLA Ops:
  0.6 4.1 %fusion = f32[768]{0:T(1024)S(1)} fusion(bf16[768,4096]{1,0:T(8,128)(2,1)} %param.4), kind=kLoop, calls=%fused_computation.2 | loop fusion | flops 9436416 | bytes 6294528 | tf_op jit(solution)/shard_map/reduce_sum | solution.py:308
  4.7 3.8 %psum.7 = f32[768]{0:T(1024)S(1)} all-reduce(f32[768]{0:T(1024)S(1)} %fusion), channel_id=1, replica_groups=mesh['row'=16,'col'=2] {'col'}, use_global_device_ids=true, to_apply=%region_1.0 | all-reduce | flops 768 | bytes 6144 | tf_op jit(solution)/shard_map/psum | solution.py:308
  8.5 8.0 %fusion.2.x_ref = bf16[768,4096]{1,0:T(8,128)(2,1)} fusion(bf16[768,4096]{1,0:T(8,128)(2,1)} %param.4, f32[4096]{0:T(1024)} %param.5, f32[768]{0:T(1024)S(1)} %add_rsqrt_fusion), kind=kLoop, calls=%fused_computation.4 | loop fusion | flops 12582912 | bytes 12602368 | tf_op jit(solution)/shard_map/convert_element_type | solution.py:310
  16.5 160.8 %gather_keys.1.left_ref.right_ref = bf16[6,14,768,128]{3,2,1,0:T(8,128)(2,1)} custom-call(bf16[768,4096]{1,0:T(8,128)(2,1)} %fusion.2.x_ref, bf16[4096,1792]{1,0:T(8,128)(2,1)} %gate_hbm.1, bf16[4096,1792]{1,0:T(8,128)(2,1)} %up_hbm.1), custom_call_target="tpu_custom_call" | custom-call | tf_op jit(solution)/shard_map/gather_keys/pallas_call | solution.py:206
  177.4 37.1 %tiles.1 = (f32[1,4,1792,1792]{3,2,1,0:T(8,128)}, f32[1,896,1792]{2,1,0:T(8,128)}) custom-call(s32[1]{0:T(128)} %bitcast.col_ref, bf16[6,14,768,128]{3,2,1,0:T(8,128)(2,1)} %gather_keys.1.left_ref.right_ref, bf16[6,14,768,128]{3,2,1,0:T(8,128)(2,1)} %gather_keys.1.left_ref.right_ref), custom_call_target="tpu_custom_call" | custom-call | tf_op jit(solution)/shard_map/tiles/pallas_call | solution.py:275
  (1 shorter events, 0.0 us)

commit v3 on v2

--- a/solution.py
+++ b/solution.py
@@ -188,12 +188,12 @@
     @pl.loop(0, chunks + 7)
     def _(t):
         stage(t, 0, multiply)
+        stage(t, 6, within)
+        stage(t, 5, sideways)
+        stage(t, 4, onward)
+        stage(t, 3, further)
+        stage(t, 2, spread)
         stage(t, 1, activate)
-        stage(t, 2, spread)
-        stage(t, 3, further)
-        stage(t, 4, onward)
-        stage(t, 5, sideways)
-        stage(t, 6, within)
         stage(t, 7, arrive)
 
 

time: 215 us -> 209 us (0.972)
  Pallas kernels: 198 us -> 192 us
    pallas_call x1, Pallas kernels: 161 us -> 155 us  [gather_keys(): pl.pallas_call(functools.partial(gather_kernel, n_row, step), out_shape=j...]
where the time goes in v3:
time: 209 us
  Pallas kernels  192 us (92%)
  other arithmetic  12.1 us (6%)
  blocking collectives  3.78 us (2%)
    pallas_call x1, Pallas kernels, gather_keys(): pl.pallas_call(functools.partial(gather_kernel, n_row, step), out_shape=j...  155 us
    pallas_call x1, Pallas kernels, tiles(): pl.pallas_call(functools.partial(tiles_kernel, scale), grid_spec=pltpu.Pr...  37.1 us
    convert_element_type x1, other arithmetic, by_routes(): normed = (wide * inverse[:, None] * norm_gain[None, :]).astype(jnp.bfloat16)  8.04 us

profile of v3, /device:TPU:25, one launch (start us, length us, event | category | flops | bytes accessed | tf_op | source)
XLA Modules:
  0.0 208.9 jit_solution(15918920187317226014)
XLA Ops:
  0.6 4.1 %fusion = f32[768]{0:T(1024)S(1)} fusion(bf16[768,4096]{1,0:T(8,128)(2,1)} %param.4), kind=kLoop, calls=%fused_computation.2 | loop fusion | flops 9436416 | bytes 6294528 | tf_op jit(solution)/shard_map/reduce_sum | solution.py:308
  4.7 3.8 %psum.7 = f32[768]{0:T(1024)S(1)} all-reduce(f32[768]{0:T(1024)S(1)} %fusion), channel_id=1, replica_groups=mesh['row'=16,'col'=2] {'col'}, use_global_device_ids=true, to_apply=%region_1.0 | all-reduce | flops 768 | bytes 6144 | tf_op jit(solution)/shard_map/psum | solution.py:308
  8.5 8.0 %fusion.2.x_ref = bf16[768,4096]{1,0:T(8,128)(2,1)} fusion(bf16[768,4096]{1,0:T(8,128)(2,1)} %param.4, f32[4096]{0:T(1024)} %param.5, f32[768]{0:T(1024)S(1)} %add_rsqrt_fusion), kind=kLoop, calls=%fused_computation.4 | loop fusion | flops 12582912 | bytes 12602368 | tf_op jit(solution)/shard_map/convert_element_type | solution.py:310
  16.5 155.3 %gather_keys.1.left_ref.right_ref = bf16[6,14,768,128]{3,2,1,0:T(8,128)(2,1)} custom-call(bf16[768,4096]{1,0:T(8,128)(2,1)} %fusion.2.x_ref, bf16[4096,1792]{1,0:T(8,128)(2,1)} %gate_hbm.1, bf16[4096,1792]{1,0:T(8,128)(2,1)} %up_hbm.1), custom_call_target="tpu_custom_call" | custom-call | tf_op jit(solution)/shard_map/gather_keys/pallas_call | solution.py:206
  171.8 37.1 %tiles.1 = (f32[1,4,1792,1792]{3,2,1,0:T(8,128)}, f32[1,896,1792]{2,1,0:T(8,128)}) custom-call(s32[1]{0:T(128)} %bitcast.col_ref, bf16[6,14,768,128]{3,2,1,0:T(8,128)(2,1)} %gather_keys.1.left_ref.right_ref, bf16[6,14,768,128]{3,2,1,0:T(8,128)(2,1)} %gather_keys.1.left_ref.right_ref), custom_call_target="tpu_custom_call" | custom-call | tf_op jit(solution)/shard_map/tiles/pallas_call | solution.py:275
  (1 shorter events, 0.0 us)
